TPU v7x, 32 devices: a whole 2x2x4 slice. The times are simulated.
32 devices in a mesh: grid: 4 (over y, core), tile: 8 (over z, x).
Axes of the slice: x: 2, y: 2, z: 4, core: 2. Of those that a mesh axis runs over, the one named last changes fastest.
Arguments:
- state_field: float32 [4, 128, 4, 4, 4, 4, 128], P('grid', 'tile'), may hold values from -6 to 6
- levels: int32 [4, 6], P('grid'), may hold values from 1 to 4
- sign_bits: int32 [4], P('grid'), may hold values from 0 to 1
Outputs:
- combined_field: float32 [4, 128, 4, 4, 4, 4, 128], P('grid', 'tile')
All inputs are finite; a program needn't handle non-finite values.
Results may differ from a plain program's by a relative error of at most 0.0003.
Values sent between devices are 32-bit elements; how exact they have to be, the bound alone decides.
A program may use at most 64 MiB of HBM per device.

v0:
```python
import functools

import jax
import jax.numpy as jnp
from jax import lax
from jax.experimental import pallas as pl
from jax.experimental.pallas import tpu as pltpu
from jax.sharding import PartitionSpec as P

STEPS = 4
ALPHA = 0.08
BETA = 0.0125


def rate_of(level):
    return jnp.where(
        level >= 4, 1.0, jnp.where(level == 3, 0.5, jnp.where(level == 2, 0.25, 0.125))
    ).astype(jnp.float32)


def kernel(
    grids, tiles, X, B,
    levels_ref, sign_ref, x_ref, o_ref,
    u0, halo_l, halo_r, pa, ma, pb, mb, val, from_pair, part, from_far, comb, out,
    load_sem, halo_send, halo_recv, pair_send, pair_recv, far_send, far_recv,
    back_send, back_recv, next_send, next_recv, store_sem,
):
    H = STEPS
    g = lax.axis_index("grid")
    t = lax.axis_index("tile")
    core = g % 2
    pair = g + 1 - 2 * core
    right = (t + 1) % tiles
    left = (t + tiles - 1) % tiles
    far = grids // 2

    def to(grid_at, tile_at):
        return {"grid": grid_at, "tile": tile_at}

    def remote(src, dst, send, recv, where):
        return pltpu.make_async_remote_copy(
            src_ref=src, dst_ref=dst, send_sem=send, recv_sem=recv,
            device_id=where, device_id_type=pl.DeviceIdType.MESH,
        )

    load = pltpu.make_async_copy(x_ref, u0, load_sem)
    load.start()

    barrier = pltpu.get_barrier_semaphore()
    others = [to(g, left), to(g, right), to(pair, t)]
    others += [to((g + 2 * k) % grids, t) for k in range(1, far)]
    for other in others:
        pl.semaphore_signal(barrier, inc=1, device_id=other, device_id_type=pl.DeviceIdType.MESH)
    pl.semaphore_wait(barrier, len(others))

    rightward = remote(x_ref.at[X - H:X], halo_l, halo_send.at[0], halo_recv.at[0], to(g, right))
    rightward.start()
    leftward = remote(x_ref.at[0:H], halo_r, halo_send.at[1], halo_recv.at[1], to(g, left))
    leftward.start()

    rates = [rate_of(levels_ref[0, d]) for d in range(6)]
    total = rates[0] + rates[1] + rates[2] + rates[3] + rates[4] + rates[5]
    centre = 1.0 / (2.0 * ALPHA) - total
    sign = (2 * sign_ref[0] - 1).astype(jnp.float32)

    blocks = 4
    sub = lax.broadcasted_iota(jnp.int32, (B, 8, 128), 1)
    low = sub < 4
    first = sub % 4 == 0
    last = sub % 4 == 3

    def split(u, p_ref, m_ref, layer, rows):
        bent = BETA * u
        p_ref[layer, rows] = u * (ALPHA - bent)
        m_ref[layer, rows] = u * (ALPHA + bent)

    def convert(src, p_ref, m_ref, start, count):
        def body(i, carry):
            layer = i // blocks
            rows = pl.ds(pl.multiple_of((i % blocks) * B, B), B)
            split(src[layer, rows], p_ref, m_ref, layer + start, rows)
            return carry
        lax.fori_loop(0, count * blocks, body, 0)

    def swapped(v):
        pieces = []
        for k in range(0, B, 2):
            pieces += [v[k + 1:k + 2], v[k:k + 1]]
        return jnp.concatenate(pieces, 0)

    def stencil(p_ref, m_ref, layer, block):
        rows = pl.ds(pl.multiple_of(block * B, B), B)
        up = pl.ds(pl.multiple_of(((block + 1) % blocks) * B, B), B)
        down = pl.ds(pl.multiple_of(((block + blocks - 1) % blocks) * B, B), B)
        p = p_ref[layer, rows]
        m = m_ref[layer, rows]
        acc = centre * (p + m)
        acc += rates[0] * (p_ref[layer + 1, rows] + m_ref[layer - 1, rows])
        acc += rates[1] * (p_ref[layer, up] + m_ref[layer, down])
        p2 = jnp.concatenate([p[2:], p[:2]], 0)
        m2 = jnp.concatenate([m[B - 2:], m[:B - 2]], 0)
        acc += rates[2] * (p2 + m2)
        ph = pltpu.roll(p, 4, 1)
        mh = pltpu.roll(m, 4, 1)
        acc += rates[3] * (jnp.where(low, ph, swapped(ph)) + jnp.where(low, swapped(mh), mh))
        p4 = pltpu.roll(jnp.where(first, ph, p), 7, 1)
        m4 = pltpu.roll(jnp.where(last, mh, m), 1, 1)
        acc += rates[4] * (p4 + m4)
        acc += rates[5] * (pltpu.roll(p, 127, 2) + pltpu.roll(m, 1, 2))
        return acc, rows

    state = [(pa, ma), (pb, mb)]

    def step(at, lo, hi):
        src, dst = state[at % 2], state[(at + 1) % 2]

        def body(i, carry):
            layer = i // blocks + (lo + H)
            acc, rows = stencil(*src, layer, i % blocks)
            if at == STEPS - 1:
                val[layer - H, rows] = sign * acc
            else:
                split(acc, *dst, layer, rows)
            return carry
        lax.fori_loop(0, (hi - lo) * blocks, body, 0)

    bases = list(range(H, X - H, H)) + [0, X - H]
    W = H // 2

    def pair_copy(j):
        return remote(
            val.at[pl.ds(bases[j] + (1 - core) * W, W)], from_pair.at[pl.ds(j * W, W)],
            pair_send.at[j], pair_recv.at[j], to(pair, t),
        )

    def far_copy(j, k):
        return remote(
            part.at[pl.ds(j * W, W)], from_far.at[k - 1, pl.ds(j * W, W)],
            far_send.at[k - 1, j], far_recv.at[k - 1, j], to((g + 2 * k) % grids, t),
        )

    def back_copy(j):
        mine = comb.at[pl.ds(bases[j] + core * W, W)]
        return remote(mine, mine, back_send.at[j], back_recv.at[j], to(pair, t))

    def reduce_pair(j):
        pair_copy(j).wait_recv()

        def body(i, carry):
            w = i // blocks
            rows = pl.ds(pl.multiple_of((i % blocks) * B, B), B)
            part[j * W + w, rows] = (
                val[bases[j] + core * W + w, rows] + from_pair[j * W + w, rows]
            )
            return carry
        lax.fori_loop(0, W * blocks, body, 0)
        for k in range(1, far):
            far_copy(j, k).start()

    def reduce_far(j):
        for k in range(1, far):
            far_copy(j, k).wait_recv()

        def body(i, carry):
            w = i // blocks
            rows = pl.ds(pl.multiple_of((i % blocks) * B, B), B)
            summed = part[j * W + w, rows]
            for k in range(1, far):
                summed += from_far[k - 1, j * W + w, rows]
            comb[bases[j] + core * W + w, rows] = summed
            return carry
        lax.fori_loop(0, W * blocks, body, 0)
        back_copy(j).start()

    inner = len(bases) - 2
    load.wait()
    convert(u0, pa, ma, H, X)
    for at in range(STEPS - 1):
        step(at, at + 1, X - at - 1)
    for j in range(inner):
        step(STEPS - 1, bases[j], bases[j] + H)
        pair_copy(j).start()
    for j in range(inner):
        reduce_pair(j)

    rightward.wait_recv()
    convert(halo_l, pa, ma, 0, H)
    for at in range(STEPS):
        step(at, at + 1 - H, at + 1)
    pair_copy(inner).start()
    reduce_pair(inner)

    leftward.wait_recv()
    convert(halo_r, pa, ma, X + H, H)
    for at in range(STEPS):
        step(at, X - at - 1, X - at - 1 + H)
    pair_copy(inner + 1).start()
    reduce_pair(inner + 1)

    for j in range(inner + 1):
        reduce_far(j)
    back_copy(inner).wait_recv()
    following = remote(comb.at[0], comb.at[X], next_send, next_recv, to(g, left))
    following.start()
    reduce_far(inner + 1)
    for j in range(inner + 2):
        if j != inner:
            back_copy(j).wait_recv()
    following.wait_recv()

    level = levels_ref[0, 0]

    def weighted(i, carry):
        layer = i // blocks
        rows = pl.ds(pl.multiple_of((i % blocks) * B, B), B)
        two, four, eight = layer // 2 * 2, layer // 4 * 4, layer // 8 * 8
        anchor = jnp.where(
            level >= 4, layer, jnp.where(level == 3, two, jnp.where(level == 2, four, eight))
        )
        spacing = jnp.where(level >= 4, 1, jnp.where(level == 3, 2, jnp.where(level == 2, 4, 8)))
        weight = (layer - anchor).astype(jnp.float32) * rates[0]
        out[layer, rows] = (1.0 - weight) * comb[anchor, rows] + weight * comb[anchor + spacing, rows]
        return carry

    stores = []
    for j in range(X // H):
        lax.fori_loop(j * H * blocks, (j + 1) * H * blocks, weighted, 0)
        store = pltpu.make_async_copy(
            out.at[pl.ds(j * H, H)], o_ref.at[pl.ds(j * H, H)], store_sem.at[j]
        )
        store.start()
        stores.append(store)

    rightward.wait_send()
    leftward.wait_send()
    for j in range(inner + 2):
        pair_copy(j).wait_send()
        for k in range(1, far):
            far_copy(j, k).wait_send()
        back_copy(j).wait_send()
    following.wait_send()
    for store in stores:
        store.wait()


def solution(mesh):
    grids, tiles = mesh.shape["grid"], mesh.shape["tile"]

    def on_device(state_field, levels, sign_bits):
        X = state_field.shape[1]
        L = state_field.shape[-1]
        V = state_field.size // (X * 8 * L)
        B = V // state_field.shape[2]
        H = STEPS
        N = X // H
        f32 = jnp.float32
        field = (V, 8, L)
        dma = pltpu.SemaphoreType.DMA
        result = pl.pallas_call(
            functools.partial(kernel, grids, tiles, X, B),
            out_shape=jax.ShapeDtypeStruct((X, *field), f32),
            in_specs=[
                pl.BlockSpec(memory_space=pltpu.SMEM),
                pl.BlockSpec(memory_space=pltpu.SMEM),
                pl.BlockSpec(memory_space=pl.ANY),
            ],
            out_specs=pl.BlockSpec(memory_space=pl.ANY),
            scratch_shapes=[
                pltpu.VMEM((X, *field), f32),
                pltpu.VMEM((H, *field), f32),
                pltpu.VMEM((H, *field), f32),
                pltpu.VMEM((X + 2 * H, *field), f32),
                pltpu.VMEM((X + 2 * H, *field), f32),
                pltpu.VMEM((X + 2 * H, *field), f32),
                pltpu.VMEM((X + 2 * H, *field), f32),
                pltpu.VMEM((X, *field), f32),
                pltpu.VMEM((X // 2, *field), f32),
                pltpu.VMEM((X // 2, *field), f32),
                pltpu.VMEM((grids // 2 - 1, X // 2, *field), f32),
                pltpu.VMEM((X + 1, *field), f32),
                pltpu.VMEM((X, *field), f32),
                dma,
                dma((2,)),
                dma((2,)),
                dma((N,)),
                dma((N,)),
                dma((grids // 2 - 1, N)),
                dma((grids // 2 - 1, N)),
                dma((N,)),
                dma((N,)),
                dma,
                dma,
                dma((N,)),
            ],
            compiler_params=pltpu.CompilerParams(
                collective_id=0, has_side_effects=True, vmem_limit_bytes=48 * 1024 * 1024
            ),
        )(levels, sign_bits, state_field.reshape(X, *field))
        return result.reshape(state_field.shape)

    placed = (P("grid", "tile", None, None, None, None, None), P("grid", None), P("grid"))
    return jax.shard_map(
        on_device,
        mesh=mesh,
        in_specs=placed,
        out_specs=P("grid", "tile", None, None, None, None, None),
        check_vma=False,
    )
```

profile of v0, /device:TPU:0, one launch (start us, length us, event | category | flops | bytes accessed | tf_op | source)
XLA Modules:
  0.0 57.4 jit_solution(3591250014536549178)
XLA Ops:
  0.7 0.0 copy-start
  0.7 1.6 %copy-done = f32[1,16,4,4,4,4,128]{6,5,4,3,2,1,0:T(4,128)S(1)} copy-done((f32[1,16,4,4,4,4,128]{6,5,4,3,2,1,0:T(4,128)S(1)}, f32[1,16,4,4,4,4,128]{6,5,4,3,2,1,0:T(4,128)}, u32[]{:S(2)}) %copy-start) | copy-done | bytes 2097176
  2.2 0.0 copy-start.1
  2.2 0.7 %copy-done.1 = s32[1,6]{1,0:T(1,128)S(1)} copy-done((s32[1,6]{1,0:T(1,128)S(1)}, s32[1,6]{1,0:T(1,128)}, u32[]{:S(2)}) %copy-start.1) | copy-done | bytes 48
  2.9 53.2 %shard_map.37 = f32[16,32,8,128]{3,2,1,0:T(8,128)S(1)} custom-call(s32[1,6]{1,0:T(1,128)S(1)} %copy-done.1, s32[1]{0:T(128)S(6)} %copy.5.sign_ref, f32[16,32,8,128]{3,2,1,0:T(8,128)S(1)} %bitcast.3), custom_call_target="tpu_custom_call" | custom-call | tf_op jit(solution)/shard_map/pallas_call | solution.py:259
  56.1 1.3 %copy.6 = f32[1,16,4,4,4,4,128]{6,5,4,3,2,1,0:T(4,128)} copy(f32[1,16,4,4,4,4,128]{6,5,4,3,2,1,0:T(4,128)S(1)} %bitcast.2) | data formatting | bytes 4194304
Async XLA Ops:
  0.7 1.6 %copy-start = (f32[1,16,4,4,4,4,128]{6,5,4,3,2,1,0:T(4,128)S(1)}, f32[1,16,4,4,4,4,128]{6,5,4,3,2,1,0:T(4,128)}, u32[]{:S(2)}) copy-start(f32[1,16,4,4,4,4,128]{6,5,4,3,2,1,0:T(4,128)} %param.3) | copy-start | bytes 6291460
  2.2 0.7 %copy-start.1 = (s32[1,6]{1,0:T(1,128)S(1)}, s32[1,6]{1,0:T(1,128)}, u32[]{:S(2)}) copy-start(s32[1,6]{1,0:T(1,128)} %levels_ref.1) | copy-start | bytes 76
where the time goes:
time: 58.3 us; the launch traced here: 57.4 us
  Pallas kernels  53.2 us (91%)
  local copies, waits for them, and re-layouts  3.56 us (6%)
  between operations  0.67 us (1%)
    pallas_call x1, Pallas kernels, on_device(): pl.pallas_call(functools.partial(kernel, grids, tiles, X, B), out_shape=j...  53.2 us
    unnamed x5, local copies, waits for them, and re-layouts  3.56 us

commit v1 on v0

v1 whole, which is shorter than its diff:
```python
import functools

import jax
import jax.numpy as jnp
from jax import lax
from jax.experimental import pallas as pl
from jax.experimental.pallas import tpu as pltpu
from jax.sharding import PartitionSpec as P

STEPS = 4
ALPHA = 0.08
BETA = 0.0125


def rate_of(level):
    return jnp.where(
        level >= 4, 1.0, jnp.where(level == 3, 0.5, jnp.where(level == 2, 0.25, 0.125))
    ).astype(jnp.float32)


def kernel(
    grids, tiles, X, B,
    levels_hbm, sign_hbm, x_ref, o_ref,
    levels_ref, sign_ref, u0, halo, pa, ma, pb, mb, val, from_pair, part, from_far, comb, after,
    load_sem, halo_send, halo_recv, pair_send, pair_recv, far_send, far_recv,
    back_send, back_recv, next_send, next_recv,
):
    H = STEPS
    g = lax.axis_index("grid")
    t = lax.axis_index("tile")
    core = g % 2
    pair = g + 1 - 2 * core
    right = (t + 1) % tiles
    left = (t + tiles - 1) % tiles
    far = grids // 2

    def to(grid_at, tile_at):
        return {"grid": grid_at, "tile": tile_at}

    def remote(src, dst, send, recv, where):
        return pltpu.make_async_remote_copy(
            src_ref=src, dst_ref=dst, send_sem=send, recv_sem=recv,
            device_id=where, device_id_type=pl.DeviceIdType.MESH,
        )

    load = pltpu.make_async_copy(x_ref, u0, load_sem.at[0])
    load.start()
    load_levels = pltpu.make_async_copy(levels_hbm, levels_ref, load_sem.at[1])
    load_levels.start()
    load_sign = pltpu.make_async_copy(sign_hbm, sign_ref, load_sem.at[2])
    load_sign.start()

    barrier = pltpu.get_barrier_semaphore()
    others = [to(g, left), to(g, right), to(pair, t)]
    others += [to((g + 2 * k) % grids, t) for k in range(1, far)]
    for other in others:
        pl.semaphore_signal(barrier, inc=1, device_id=other, device_id_type=pl.DeviceIdType.MESH)
    pl.semaphore_wait(barrier, len(others))

    lead = t % 2

    def outward(side, k):
        return remote(
            x_ref.at[k + side * (X - 1 - 2 * k)], halo.at[1 - side, k],
            halo_send.at[side, k], halo_recv.at[1 - side, k],
            to(g, (t + tiles - 1 + 2 * side) % tiles),
        )

    for k in range(H):
        outward(lead, k).start()
    for k in range(H):
        outward(1 - lead, k).start()
    load_levels.wait()
    load_sign.wait()

    rates = [rate_of(levels_ref[0, d]) for d in range(6)]
    total = rates[0] + rates[1] + rates[2] + rates[3] + rates[4] + rates[5]
    centre = 1.0 / (2.0 * ALPHA) - total
    sign = (2 * sign_ref[0] - 1).astype(jnp.float32)

    blocks = 4
    sub = lax.broadcasted_iota(jnp.int32, (B, 8, 128), 1)
    low = sub < 4
    first = sub % 4 == 0
    last = sub % 4 == 3

    def split(u, p_ref, m_ref, layer, rows):
        bent = BETA * u
        p_ref[layer, rows] = u * (ALPHA - bent)
        m_ref[layer, rows] = u * (ALPHA + bent)

    def convert(src, p_ref, m_ref, layer):
        def body(i, carry):
            rows = pl.ds(pl.multiple_of(i * B, B), B)
            split(src[rows], p_ref, m_ref, layer, rows)
            return carry
        lax.fori_loop(0, blocks, body, 0)

    sub = lax.broadcasted_iota(jnp.int32, (2, 8, 128), 1)
    low = sub < 4
    first = sub % 4 == 0
    last = sub % 4 == 3
    fine = blocks * blocks

    def swapped(v):
        return jnp.concatenate([v[1:2], v[0:1]], 0)

    def at_rows(i):
        return pl.ds(i * 2, 2)

    def stencil(p_ref, m_ref, layer, i):
        rows = at_rows(i)
        p = p_ref[layer, rows]
        m = m_ref[layer, rows]
        p5 = pltpu.roll(p, 127, 2)
        m5 = pltpu.roll(m, 1, 2)
        acc = centre * (p + m)
        acc += rates[0] * (p_ref[layer + 1, rows] + m_ref[layer - 1, rows])
        i1, i2 = i // blocks * blocks, i % blocks
        acc += rates[1] * (
            p_ref[layer, at_rows((i + blocks) % fine)]
            + m_ref[layer, at_rows((i + fine - blocks) % fine)]
        )
        acc += rates[2] * (
            p_ref[layer, at_rows(i1 + (i2 + 1) % blocks)]
            + m_ref[layer, at_rows(i1 + (i2 + blocks - 1) % blocks)]
        )
        ph = pltpu.roll(p, 4, 1)
        mh = pltpu.roll(m, 4, 1)
        acc += rates[3] * (jnp.where(low, ph, swapped(ph)) + jnp.where(low, swapped(mh), mh))
        p4 = pltpu.roll(jnp.where(first, ph, p), 7, 1)
        m4 = pltpu.roll(jnp.where(last, mh, m), 1, 1)
        acc += rates[4] * (p4 + m4)
        acc += rates[5] * (p5 + m5)
        return acc, rows

    state = [(pa, ma), (pb, mb)]

    def step(at, lo, count):
        src, dst = state[at % 2], state[(at + 1) % 2]

        def body(i, carry):
            layer = i + (lo + H)
            for n in range(fine):
                acc, rows = stencil(*src, layer, n)
                if at == STEPS - 1:
                    val[layer - H, rows] = sign * acc
                else:
                    split(acc, *dst, layer, rows)
            return carry
        lax.fori_loop(0, count, body, 0)

    chunks = [(at, H) for at in range(H, X - H, H)]
    inner = len(chunks)
    W = H // 2
    for side in (lead, 1 - lead):
        for q in range(2):
            near = H - (q + 1) * W
            chunks.append((near + side * (X - W - 2 * near), W))
    half = B * blocks // 2
    mine = pl.ds(pl.multiple_of(core * half, half), half)
    theirs = pl.ds(pl.multiple_of((1 - core) * half, half), half)

    def layers(j):
        return pl.ds(chunks[j][0], chunks[j][1])

    def pair_copy(j):
        return remote(
            val.at[layers(j), theirs], from_pair.at[layers(j)],
            pair_send.at[j], pair_recv.at[j], to(pair, t),
        )

    def far_copy(j, k):
        return remote(
            part.at[layers(j)], from_far.at[k - 1, layers(j)],
            far_send.at[k - 1, j], far_recv.at[k - 1, j], to((g + 2 * k) % grids, t),
        )

    def back_copy(j):
        own = comb.at[layers(j), mine]
        return remote(own, own, back_send.at[j], back_recv.at[j], to(pair, t))

    def reduce_pair(j):
        pair_copy(j).wait_recv()

        def body(w, carry):
            i = chunks[j][0] + w
            part[i] = val[i, mine] + from_pair[i]
            return carry
        lax.fori_loop(0, chunks[j][1], body, 0)
        for k in range(1, far):
            far_copy(j, k).start()

    def reduce_far(j):
        for k in range(1, far):
            far_copy(j, k).wait_recv()

        def body(w, carry):
            i = chunks[j][0] + w
            summed = part[i]
            for k in range(1, far):
                summed += from_far[k - 1, i]
            comb[i, mine] = summed
            return carry
        lax.fori_loop(0, chunks[j][1], body, 0)
        back_copy(j).start()

    def front(side, lo, hi):
        def mirrored(at):
            return at + side * (X - 1 - 2 * at)

        def wave(k, carry):
            outward(1 - side, k).wait_recv()
            convert(halo.at[side, k], pa, ma, H + mirrored(-1 - k))
            for at in range(STEPS):
                step(at, mirrored(at - k), 1)
            return carry
        lax.fori_loop(lo, hi, wave, 0)

    load.wait()

    def convert_all(i, carry):
        convert(u0.at[i], pa, ma, i + H)
        return carry
    lax.fori_loop(0, X, convert_all, 0)

    for at in range(STEPS):
        step(at, at + 1, 3 * H - 2 - 2 * at)
    pair_copy(0).start()
    for j in range(1, inner):
        for at in range(STEPS):
            step(at, chunks[j][0] + H - 1 - at, H)
            if j == 1 and at == 0:
                reduce_pair(0)
        pair_copy(j).start()
        if j > 1:
            reduce_pair(j - 1)
    front(lead, 0, W)
    pair_copy(inner).start()
    reduce_pair(inner - 1)
    front(lead, W, H)
    pair_copy(inner + 1).start()
    reduce_pair(inner)
    front(1 - lead, 0, W)
    pair_copy(inner + 2).start()
    reduce_pair(inner + 1)
    reduce_far(0)
    front(1 - lead, W, H)
    pair_copy(inner + 3).start()
    reduce_pair(inner + 2)
    for j in range(1, inner):
        reduce_far(j)
    reduce_pair(inner + 3)
    reduce_far(inner)
    reduce_far(inner + 1)
    following = remote(comb.at[0], after, next_send, next_recv, to(g, left))
    back_copy(inner + 1).wait_recv()

    @pl.when(lead == 0)
    def _():
        following.start()

    reduce_far(inner + 2)
    reduce_far(inner + 3)
    back_copy(inner + 3).wait_recv()

    @pl.when(lead == 1)
    def _():
        following.start()

    for j in list(range(inner + 1)) + [inner + 2]:
        back_copy(j).wait_recv()

    level = levels_ref[0, 0]

    def weighted(i, carry):
        layer = i // blocks
        rows = pl.ds(pl.multiple_of((i % blocks) * B, B), B)
        two, four, eight = layer // 2 * 2, layer // 4 * 4, layer // 8 * 8
        anchor = jnp.where(
            level >= 4, layer, jnp.where(level == 3, two, jnp.where(level == 2, four, eight))
        )
        spacing = jnp.where(level >= 4, 1, jnp.where(level == 3, 2, jnp.where(level == 2, 4, 8)))
        weight = (layer - anchor).astype(jnp.float32) * rates[0]
        o_ref[layer, rows] = (1.0 - weight) * comb[anchor, rows] + weight * comb[anchor + spacing, rows]
        return carry

    reach = 8
    lax.fori_loop(0, (X - reach) * blocks, weighted, 0)
    following.wait_recv()
    comb[X] = after[...]
    lax.fori_loop((X - reach) * blocks, X * blocks, weighted, 0)

    for k in range(H):
        outward(0, k).wait_send()
        outward(1, k).wait_send()
    for j in range(inner + 4):
        pair_copy(j).wait_send()
        for k in range(1, far):
            far_copy(j, k).wait_send()
        back_copy(j).wait_send()
    following.wait_send()


def solution(mesh):
    grids, tiles = mesh.shape["grid"], mesh.shape["tile"]

    def on_device(state_field, levels, sign_bits):
        X = state_field.shape[1]
        L = state_field.shape[-1]
        V = state_field.size // (X * 8 * L)
        B = V // state_field.shape[2]
        H = STEPS
        N = X // H + 2
        far = grids // 2 - 1
        f32 = jnp.float32
        field = (V, 8, L)
        halved = (V // 2, 8, L)
        dma = pltpu.SemaphoreType.DMA
        result = pl.pallas_call(
            functools.partial(kernel, grids, tiles, X, B),
            out_shape=jax.ShapeDtypeStruct((X, *field), f32),
            in_specs=[pl.BlockSpec(memory_space=pltpu.HBM)] * 3,
            out_specs=pl.BlockSpec(memory_space=pltpu.VMEM),
            scratch_shapes=[
                pltpu.SMEM(levels.shape, jnp.int32),
                pltpu.SMEM(sign_bits.shape, jnp.int32),
                pltpu.VMEM((X, *field), f32),
                pltpu.VMEM((2, H, *field), f32),
                pltpu.VMEM((X + 2 * H, *field), f32),
                pltpu.VMEM((X + 2 * H, *field), f32),
                pltpu.VMEM((X + 2 * H, *field), f32),
                pltpu.VMEM((X + 2 * H, *field), f32),
                pltpu.VMEM((X, *field), f32),
                pltpu.VMEM((X, *halved), f32),
                pltpu.VMEM((X, *halved), f32),
                pltpu.VMEM((far, X, *halved), f32),
                pltpu.VMEM((X + 1, *field), f32),
                pltpu.VMEM(field, f32),
                dma((3,)),
                dma((2, H)),
                dma((2, H)),
                dma((N,)),
                dma((N,)),
                dma((far, N)),
                dma((far, N)),
                dma((N,)),
                dma((N,)),
                dma,
                dma,
            ],
            compiler_params=pltpu.CompilerParams(
                collective_id=0, has_side_effects=True, vmem_limit_bytes=48 * 1024 * 1024
            ),
        )(levels, sign_bits, state_field.reshape(X, *field))
        return result.reshape(state_field.shape)

    placed = (P("grid", "tile", None, None, None, None, None), P("grid", None), P("grid"))
    return jax.shard_map(
        on_device,
        mesh=mesh,
        in_specs=placed,
        out_specs=P("grid", "tile", None, None, None, None, None),
        check_vma=False,
    )
```

time: 58.3 us -> 47.8 us (0.82); the launches traced: 57.4 us -> 47.6 us
  Pallas kernels: 53.2 us -> 43.4 us
    pallas_call x1, Pallas kernels: 53.2 us -> 43.4 us  [on_device(): pl.pallas_call(functools.partial(kernel, grids, tiles, X, B), out_shape=j...]
where the time goes in v1:
time: 47.8 us; the launch traced here: 47.6 us
  Pallas kernels  43.4 us (91%)
  local copies, waits for them, and re-layouts  3.56 us (7%)
  between operations  0.67 us (1%)
    pallas_call x1, Pallas kernels, on_device(): pl.pallas_call(functools.partial(kernel, grids, tiles, X, B), out_shape=j...  43.4 us
    unnamed x5, local copies, waits for them, and re-layouts  3.56 us

profile of v1, /device:TPU:0, one launch (start us, length us, event | category | flops | bytes accessed | tf_op | source)
XLA Modules:
  0.0 47.6 jit_solution(9736996767615430599)
XLA Ops:
  0.7 0.0 copy-start
  0.7 1.6 %copy-done = f32[1,16,4,4,4,4,128]{6,5,4,3,2,1,0:T(4,128)S(1)} copy-done((f32[1,16,4,4,4,4,128]{6,5,4,3,2,1,0:T(4,128)S(1)}, f32[1,16,4,4,4,4,128]{6,5,4,3,2,1,0:T(4,128)}, u32[]{:S(2)}) %copy-start) | copy-done | bytes 2097176
  2.2 0.0 copy-start.1
  2.2 0.7 %copy-done.1 = s32[1,6]{1,0:T(1,128)S(1)} copy-done((s32[1,6]{1,0:T(1,128)S(1)}, s32[1,6]{1,0:T(1,128)}, u32[]{:S(2)}) %copy-start.1) | copy-done | bytes 48
  2.9 43.4 %shard_map.37 = f32[16,32,8,128]{3,2,1,0:T(8,128)S(1)} custom-call(s32[1,6]{1,0:T(1,128)S(1)} %copy-done.1, s32[1]{0:T(128)S(6)} %copy.5.sign_hbm, f32[16,32,8,128]{3,2,1,0:T(8,128)S(1)} %bitcast.3), custom_call_target="tpu_custom_call" | custom-call | tf_op jit(solution)/shard_map/pallas_call | solution.py:320
  46.3 1.3 %copy.6 = f32[1,16,4,4,4,4,128]{6,5,4,3,2,1,0:T(4,128)} copy(f32[1,16,4,4,4,4,128]{6,5,4,3,2,1,0:T(4,128)S(1)} %bitcast.2) | data formatting | bytes 4194304
Async XLA Ops:
  0.7 1.6 %copy-start = (f32[1,16,4,4,4,4,128]{6,5,4,3,2,1,0:T(4,128)S(1)}, f32[1,16,4,4,4,4,128]{6,5,4,3,2,1,0:T(4,128)}, u32[]{:S(2)}) copy-start(f32[1,16,4,4,4,4,128]{6,5,4,3,2,1,0:T(4,128)} %param.3) | copy-start | bytes 6291460
  2.2 0.7 %copy-start.1 = (s32[1,6]{1,0:T(1,128)S(1)}, s32[1,6]{1,0:T(1,128)}, u32[]{:S(2)}) copy-start(s32[1,6]{1,0:T(1,128)} %levels_hbm.1) | copy-start | bytes 76

commit v2 on v1

--- a/solution.py
+++ b/solution.py
@@ -286,10 +286,10 @@
         return carry
 
     reach = 8
-    lax.fori_loop(0, (X - reach) * blocks, weighted, 0)
+    lax.fori_loop(0, (X - reach) * blocks, weighted, 0, unroll=4)
     following.wait_recv()
     comb[X] = after[...]
-    lax.fori_loop((X - reach) * blocks, X * blocks, weighted, 0)
+    lax.fori_loop((X - reach) * blocks, X * blocks, weighted, 0, unroll=4)
 
     for k in range(H):
         outward(0, k).wait_send()

time: 47.8 us -> 47.6 us (level)
  no operation moved by 1% of the time
where the time goes in v2:
time: 47.6 us; the launch traced here: 47.4 us
  Pallas kernels  43.2 us (91%)
  local copies, waits for them, and re-layouts  3.56 us (7%)
  between operations  0.67 us (1%)
    pallas_call x1, Pallas kernels, on_device(): pl.pallas_call(functools.partial(kernel, grids, tiles, X, B), out_shape=j...  43.2 us
    unnamed x5, local copies, waits for them, and re-layouts  3.56 us

profile of v2, /device:TPU:0, one launch (start us, length us, event | category | flops | bytes accessed | tf_op | source)
XLA Modules:
  0.0 47.4 jit_solution(12576546412440554180)
XLA Ops:
  0.7 0.0 copy-start
  0.7 1.6 %copy-done = f32[1,16,4,4,4,4,128]{6,5,4,3,2,1,0:T(4,128)S(1)} copy-done((f32[1,16,4,4,4,4,128]{6,5,4,3,2,1,0:T(4,128)S(1)}, f32[1,16,4,4,4,4,128]{6,5,4,3,2,1,0:T(4,128)}, u32[]{:S(2)}) %copy-start) | copy-done | bytes 2097176
  2.2 0.0 copy-start.1
  2.2 0.7 %copy-done.1 = s32[1,6]{1,0:T(1,128)S(1)} copy-done((s32[1,6]{1,0:T(1,128)S(1)}, s32[1,6]{1,0:T(1,128)}, u32[]{:S(2)}) %copy-start.1) | copy-done | bytes 48
  2.9 43.2 %shard_map.37 = f32[16,32,8,128]{3,2,1,0:T(8,128)S(1)} custom-call(s32[1,6]{1,0:T(1,128)S(1)} %copy-done.1, s32[1]{0:T(128)S(6)} %copy.5.sign_hbm, f32[16,32,8,128]{3,2,1,0:T(8,128)S(1)} %bitcast.3), custom_call_target="tpu_custom_call" | custom-call | tf_op jit(solution)/shard_map/pallas_call | solution.py:320
  46.1 1.3 %copy.6 = f32[1,16,4,4,4,4,128]{6,5,4,3,2,1,0:T(4,128)} copy(f32[1,16,4,4,4,4,128]{6,5,4,3,2,1,0:T(4,128)S(1)} %bitcast.2) | data formatting | bytes 4194304
Async XLA Ops:
  0.7 1.6 %copy-start = (f32[1,16,4,4,4,4,128]{6,5,4,3,2,1,0:T(4,128)S(1)}, f32[1,16,4,4,4,4,128]{6,5,4,3,2,1,0:T(4,128)}, u32[]{:S(2)}) copy-start(f32[1,16,4,4,4,4,128]{6,5,4,3,2,1,0:T(4,128)} %param.3) | copy-start | bytes 6291460
  2.2 0.7 %copy-start.1 = (s32[1,6]{1,0:T(1,128)S(1)}, s32[1,6]{1,0:T(1,128)}, u32[]{:S(2)}) copy-start(s32[1,6]{1,0:T(1,128)} %levels_hbm.1) | copy-start | bytes 76
